TPU v7x, 128 devices: a whole 4x4x4 slice. The times are simulated.
128 devices in a mesh: seq: 16 (over y_lo, x, core), cb: 8 (over y_hi, z).
Axes of the slice: x: 4, y: 4 (y_hi: 2, y_lo: 2; y = y_hi * 2 + y_lo), z: 4, core: 2. Of those that a mesh axis runs over, the one named last changes fastest.
Arguments:
- hidden: bfloat16 [2, 2048, 4096], P(None, 'seq'), may hold values from -6 to 6
- temporal_gain: float32 [4096], replicated, may hold values from 0.5 to 2
- temporal_qkv: bfloat16 [3, 4096, 2048], P(None, None, 'cb'), may hold values from -10 to 10
- temporal_out: bfloat16 [2048, 4096], P('cb'), may hold values from -0.125 to 0.125
- codebook_ids: int32 [2, 2048, 8], P(None, 'seq', 'cb'), may hold values from 0 to 2047
- embedding: bfloat16 [8, 2048, 1024], P('cb'), may hold values from -6 to 6
- input_weight: bfloat16 [8, 4096, 1024], P('cb', 'seq'), may hold values from -0.09375 to 0.09375
- depth_gain: float32 [8, 1024], P('cb'), may hold values from 0.5 to 2
- depth_qkv: bfloat16 [8, 3, 1024, 1024], P('cb'), may hold values from -10 to 10
- depth_out: bfloat16 [8, 1024, 1024], P('cb'), may hold values from -0.1875 to 0.1875
Outputs:
- temporal: bfloat16 [2, 2048, 4096], P(None, 'seq')
- depth: bfloat16 [2, 2048, 8, 1024], P(None, 'seq', 'cb')
All inputs are finite; a program needn't handle non-finite values.
Results may differ from a plain program's by a relative error of at most 0.017.
Values may be sent and summed in bfloat16 or wider, within the bound.
A program may use at most 128 MiB of HBM per device.

v0:
```python
import jax
import jax.numpy as jnp
from jax import lax
from jax.sharding import PartitionSpec as P

HD = 128
DW = 1024
DH = 16
DHD = 64


def normalize(values, scale):
    mean_sq = jnp.mean(values * values, axis=-1, keepdims=True)
    return values * lax.rsqrt(mean_sq + 1e-05) * scale


def shards(
    hidden,
    temporal_gain,
    temporal_qkv,
    temporal_out,
    codebook_ids,
    embedding,
    input_weight,
    depth_gain,
    depth_qkv,
    depth_out,
):
    seq_count, frames, width = hidden.shape
    head_cols = temporal_qkv.shape[2]
    head_count = head_cols // HD
    row_count = seq_count * frames
    hidden_f = hidden.astype(jnp.float32)
    normed = normalize(hidden_f, temporal_gain).astype(jnp.bfloat16).reshape(row_count, width)
    projected = []
    for which in range(3):
        part_rows = jnp.dot(normed, temporal_qkv[which], preferred_element_type=jnp.float32).astype(
            jnp.bfloat16
        )
        projected.append(part_rows.reshape(seq_count, frames, head_count, HD))
    queries = projected[0]
    query_pos = lax.axis_index("seq") * frames + jnp.arange(frames, dtype=jnp.int32)
    temporal_scale = 1.0 / jnp.sqrt(jnp.float32(HD))
    highest = jnp.full((seq_count, head_count, frames), -1e30, jnp.float32)
    key_piece = lax.all_gather(projected[1], "seq", axis=1, tiled=True)
    value_piece = lax.all_gather(projected[2], "seq", axis=1, tiled=True)
    count = key_piece.shape[1]
    scores = (
        jnp.einsum("sqhd,skhd->shqk", queries, key_piece, preferred_element_type=jnp.float32)
        * temporal_scale
    )
    key_pos = jnp.arange(count, dtype=jnp.int32)
    allowed = (key_pos[None, :] <= query_pos[:, None])[None, None]
    scores = jnp.where(allowed, scores, -1e30)
    new_high = jnp.maximum(highest, jnp.max(scores, axis=-1))
    weights = jnp.where(allowed, jnp.exp(scores - new_high[..., None]), 0.0)
    totals = jnp.sum(weights, axis=-1)
    update = jnp.einsum(
        "shqk,skhd->sqhd",
        weights.astype(jnp.bfloat16),
        value_piece,
        preferred_element_type=jnp.float32,
    )
    gathered = update
    highest, totals, gathered = (new_high, totals, gathered)
    mixed = (
        (gathered / totals.transpose(0, 2, 1)[..., None])
        .astype(jnp.bfloat16)
        .reshape(row_count, head_cols)
    )
    term = jnp.dot(mixed, temporal_out, preferred_element_type=jnp.float32)
    summed = lax.psum(term.astype(jnp.bfloat16), "cb").astype(jnp.float32)
    temporal = (hidden_f.reshape(row_count, width) + summed).astype(jnp.bfloat16)
    projected_in = jnp.dot(
        temporal,
        lax.all_gather(input_weight, "seq", axis=1, tiled=True)[0],
        preferred_element_type=jnp.float32,
    )
    entry = jnp.take(embedding[0], codebook_ids.reshape(row_count), axis=0).astype(jnp.float32)
    stream = (projected_in + entry).astype(jnp.bfloat16)
    depth_normed = normalize(stream.astype(jnp.float32), depth_gain[0]).astype(jnp.bfloat16)
    book_query = jnp.dot(depth_normed, depth_qkv[0, 0], preferred_element_type=jnp.float32).astype(
        jnp.bfloat16
    )
    book_key = jnp.dot(depth_normed, depth_qkv[0, 1], preferred_element_type=jnp.float32).astype(
        jnp.bfloat16
    )
    book_value = jnp.dot(depth_normed, depth_qkv[0, 2], preferred_element_type=jnp.float32).astype(
        jnp.bfloat16
    )
    depth_scale = 1.0 / jnp.sqrt(jnp.float32(DHD))
    my_book = lax.axis_index("cb")
    query_heads = book_query.reshape(row_count, DH, DHD)
    highest_b = jnp.full((row_count, DH), -1e30, jnp.float32)
    key_piece = lax.all_gather(book_key[None], "cb", axis=0, tiled=True)
    value_piece = lax.all_gather(book_value[None], "cb", axis=0, tiled=True)
    count = key_piece.shape[0]
    key_heads = key_piece.reshape(count, row_count, DH, DHD)
    value_heads = value_piece.reshape(count, row_count, DH, DHD)
    scores = (
        jnp.einsum("rhd,jrhd->rhj", query_heads, key_heads, preferred_element_type=jnp.float32)
        * depth_scale
    )
    permitted = (jnp.arange(count, dtype=jnp.int32) <= my_book)[None, None, :]
    scores = jnp.where(permitted, scores, -1e30)
    new_high = jnp.maximum(highest_b, jnp.max(scores, axis=-1))
    weights = jnp.where(permitted, jnp.exp(scores - new_high[..., None]), 0.0)
    totals_b = jnp.sum(weights, axis=-1)
    update = jnp.einsum(
        "rhj,jrhd->rhd",
        weights.astype(jnp.bfloat16),
        value_heads,
        preferred_element_type=jnp.float32,
    )
    highest_b, totals_b, gathered_b = (new_high, totals_b, update)
    book_mixed = (gathered_b / totals_b[..., None]).astype(jnp.bfloat16).reshape(row_count, DW)
    depth = (
        jnp.dot(book_mixed, depth_out[0], preferred_element_type=jnp.float32)
        + stream.astype(jnp.float32)
    ).astype(jnp.bfloat16)
    return (temporal.reshape(seq_count, frames, width), depth.reshape(seq_count, frames, 1, DW))


def solution(mesh):
    placed = (
        P(None, "seq", None),
        P(),
        P(None, None, "cb"),
        P("cb", None),
        P(None, "seq", "cb"),
        P("cb", None, None),
        P("cb", "seq", None),
        P("cb", None),
        P("cb", None, None, None),
        P("cb", None, None),
    )
    return jax.shard_map(
        shards,
        mesh=mesh,
        in_specs=placed,
        out_specs=(P(None, "seq", None), P(None, "seq", "cb", None)),
        check_vma=False,
    )
```

profile of v0, /device:TPU:1, one launch (start us, length us, event | category | flops | bytes accessed | tf_op | source)
XLA Modules:
  0.0 419.6 jit_solution(1029900267491474171)
XLA Ops:
  7.2 0.0 all-gather.10.cloned.1.call-start
  7.2 2.2 multiply_reduce_fusion.2
  9.5 2.3 multiply_convert_fusion
  11.8 1.3 copy-done.5
  13.1 2.3 fusion.58
  15.5 0.7 copy.25
  16.2 0.0 all-gather.10.cloned.1.call-update
  16.2 0.0 all-gather.8.cloned.1.call-start
  16.3 2.9 fusion.52
  19.2 0.8 copy.24
  20.0 0.0 all-gather.8.cloned.1.call-update
  20.0 0.0 all-reduce.2.cloned.1.call-start
  20.1 2.9 fusion.55
  23.1 0.2 iota_compare_fusion
  23.3 30.6 %all-gather.10.cloned.1.call-done = bf16[2,2048,2,128]{3,1,2,0:T(8,128)(2,1)} async-done(((bf16[2,128,2,128]{3,1,2,0:T(8,128)(2,1)}), bf16[2,2048,2,128]{3,1,2,0:T(8,128)(2,1)}) %all-gather.10.cloned.1.call-update) | async-done | bytes 2097168 | tf_op jit(solution)/shard_map/all_gather | solution.py:45
  53.9 2.6 fusion.3
  56.6 1.9 copy-done.3
  58.5 1.3 fusion.4
  59.7 33.6 %all-gather.8.cloned.1.call-done = bf16[2,2048,2,128]{1,3,2,0:T(8,128)(2,1)} async-done(((bf16[2,128,2,128]{1,3,2,0:T(8,128)(2,1)}), bf16[2,2048,2,128]{1,3,2,0:T(8,128)(2,1)}) %all-gather.8.cloned.1.call-update) | async-done | bytes 2097168 | tf_op jit(solution)/shard_map/all_gather | solution.py:46
  93.4 4.1 fusion.64
  97.5 0.1 copy.27
  97.6 2.0 convolution_convert_fusion
  99.7 0.0 all-gather.12.cloned.1.call-start
  99.8 0.5 all-gather.12.cloned.1.call-update
  100.3 0.2 all-gather.14.cloned.1.call-start
  100.6 4.3 %gather_fusion = bf16[256,1024]{1,0:T(8,128)(2,1)S(1)} fusion(bf16[2048,1024]{1,0:T(8,128)(2,1)} %bitcast.102, s32[1024]{0:T(1024)S(1)} %pad_clamp_fusion), kind=kCustom, calls=%fused_computation | custom fusion | bytes 1049600 | tf_op jit(solution)/shard_map/jit(_take)/gather | solution.py:79
  104.9 82.8 %all-reduce.2.cloned.1.call-done = bf16[256,4096]{1,0:T(8,128)(2,1)} async-done(((bf16[256,4096]{1,0:T(8,128)(2,1)}), bf16[256,4096]{1,0:T(8,128)(2,1)}) %all-reduce.2.cloned.1.call-update) | async-done | bytes 2097168 | tf_op jit(solution)/shard_map/psum | solution.py:72
  187.7 3.7 fusion.2
  191.4 53.9 %all-gather.12.cloned.1.call-done = bf16[1,4096,1024]{2,1,0:T(8,128)(2,1)} async-done(((bf16[1,256,1024]{2,1,0:T(8,128)(2,1)}), bf16[1,4096,1024]{2,1,0:T(8,128)(2,1)}) %all-gather.12.cloned.1.call-update) | async-done | bytes 8388624 | tf_op jit(solution)/shard_map/all_gather | solution.py:76
  245.2 6.5 %fusion.67 = (f32[256]{0:T(256)S(1)}, bf16[256,1024]{1,0:T(8,128)(2,1)S(1)}) fusion(bf16[256,1024]{1,0:T(8,128)(2,1)S(1)} %gather_fusion, pred[256]{0:T(512)(128)(4,1)S(1)} %compare_and_fusion, bf16[256,4096]{1,0:T(8,128)(2,1)} %fusion.2, bf16[1,4096,1024]{2,1,0:T(8,128)(2,1)} %all-gather.12.cloned.1.call-done), kind=kOutput, calls=%fused_computation.52 | convolution fusion | flops 2149318400 | bytes 11535616 | tf_op jit(solution)/shard_map/dot_general | solution.py:74
  251.7 3.1 fusion.43
  254.9 0.3 all-gather.16.cloned.1.call-start
  255.1 3.2 fusion.46
  258.4 2.4 fusion.40
  260.7 0.2 copy.28
  260.9 0.1 bitcast_convert_fusion
  261.1 65.6 %all-gather.14.cloned.1.call-done = bf16[2048,1024]{1,0:T(8,128)(2,1)} async-done(((bf16[256,1024]{1,0:T(8,128)(2,1)}), bf16[2048,1024]{1,0:T(8,128)(2,1)}) %all-gather.14.cloned.1.call-update) | async-done | bytes 4194320 | tf_op jit(solution)/shard_map/all_gather | solution.py:95
  326.7 6.5 %copy.29 = bf16[2048,1024]{0,1:T(8,128)(2,1)} copy(bf16[2048,1024]{1,0:T(8,128)(2,1)} %all-gather.14.cloned.1.call-done) | data formatting | bytes 8388608 | tf_op jit(solution)/shard_map/all_gather | solution.py:95
  333.1 3.7 copy.47
  336.8 0.9 multiply_reduce_fusion.1
  337.8 0.1 fusion.74
  337.9 0.1 fusion.75
  338.0 60.2 %all-gather.16.cloned.1.call-done = bf16[2048,1024]{1,0:T(8,128)(2,1)} async-done(((bf16[256,1024]{1,0:T(8,128)(2,1)}), bf16[2048,1024]{1,0:T(8,128)(2,1)}) %all-gather.16.cloned.1.call-update) | async-done | bytes 4194320 | tf_op jit(solution)/shard_map/all_gather | solution.py:96
  398.2 6.5 %copy.30 = bf16[2048,1024]{0,1:T(8,128)(2,1)} copy(bf16[2048,1024]{1,0:T(8,128)(2,1)} %all-gather.16.cloned.1.call-done) | data formatting | bytes 8388608 | tf_op jit(solution)/shard_map/all_gather | solution.py:96
  404.7 3.7 copy.48
  408.4 2.6 multiply_reduce_fusion
  411.1 0.1 divide_convert_fusion
  411.2 1.5 fusion.37
  (29 shorter events, 0.3 us)
Async XLA Ops:
  7.2 90.5 %copy-start = (bf16[256,4096]{1,0:T(8,128)(2,1)S(1)}, bf16[256,4096]{1,0:T(8,128)(2,1)}, u32[]{:S(2)}) copy-start(bf16[256,4096]{1,0:T(8,128)(2,1)} %param.13) | copy-start | bytes 6291460
  7.2 46.7 %all-gather.10.cloned.1.call-start = ((), (), s32[]{:S(2)}) async-start(), calls=%async_computation.1 | async-start | bytes 2228224 | tf_op jit(solution)/shard_map/all_gather | solution.py:45
  11.8 1.3 copy-start.5
  16.2 77.2 %all-gather.8.cloned.1.call-start = ((), (), s32[]{:S(2)}) async-start(), calls=%async_computation | async-start | bytes 2228224 | tf_op jit(solution)/shard_map/all_gather | solution.py:46
  20.0 167.7 %all-reduce.2.cloned.1.call-start = ((), (), s32[]{:S(2)}) async-start(), calls=%async_computation.2 | async-start | bytes 4194304 | tf_op jit(solution)/shard_map/psum | solution.py:72
  56.5 1.9 copy-start.3
  97.5 3.0 copy-start.6
  99.7 88.0 %copy-start.2 = (bf16[2,128,4096]{2,1,0:T(8,128)(2,1)S(1)}, bf16[2,128,4096]{2,1,0:T(8,128)(2,1)}, u32[]{:S(2)}) copy-start(bf16[2,128,4096]{2,1,0:T(8,128)(2,1)} %param.10) | copy-start | bytes 6291460
  99.7 145.5 %all-gather.12.cloned.1.call-start = ((), (), s32[]{:S(2)}) async-start(), calls=%async_computation.3 | async-start | bytes 8912896 | tf_op jit(solution)/shard_map/all_gather | solution.py:76
  100.3 226.4 %all-gather.14.cloned.1.call-start = ((), (), s32[]{:S(2)}) async-start(), calls=%async_computation.4 | async-start | bytes 4718592 | tf_op jit(solution)/shard_map/all_gather | solution.py:95
  191.4 60.3 %copy-start.7 = (f32[1,1024]{1,0:T(1,128)S(1)}, f32[1,1024]{1,0:T(1,128)}, u32[]{:S(2)}) copy-start(f32[1,1024]{1,0:T(1,128)} %param.17) | copy-start | bytes 12292
  254.9 143.3 %all-gather.16.cloned.1.call-start = ((), (), s32[]{:S(2)}) async-start(), calls=%async_computation.5 | async-start | bytes 4718592 | tf_op jit(solution)/shard_map/all_gather | solution.py:96
  408.4 2.8 copy-start.4
  408.4 4.3 %copy-start.1 = (bf16[256,4096]{1,0:T(8,128)(2,1)S(1)}, bf16[256,4096]{1,0:T(8,128)(2,1)}, u32[]{:S(2)}) copy-start(bf16[256,4096]{1,0:T(8,128)(2,1)} %param.13) | copy-start | bytes 6291460
Sparse Core Ops, SparseCore 0:
  16.3 37.5 all-gather.9
  56.1 37.2 all-gather.7
  99.8 87.8 all-reduce.1
  189.2 55.9 all-gather.11
  255.0 71.6 all-gather.13
  328.9 69.2 all-gather.15
where the time goes:
time: 420 us
  waiting for transfers between devices  327 us (78%)
  matrix products  33.6 us (8%)
  local copies, waits for them, and re-layouts  29.8 us (7%)
  between operations  14.4 us (3%)
  other arithmetic  13.8 us (3%)
    psum x1, waiting for transfers between devices, shards(): summed = lax.psum(term.astype(jnp.bfloat16), 'cb').astype(jnp.float32)  82.8 us
    all_gather x1, waiting for transfers between devices, shards(): key_piece = lax.all_gather(book_key[None], 'cb', axis=0, tiled=True)  65.6 us
    all_gather x1, waiting for transfers between devices, shards(): value_piece = lax.all_gather(book_value[None], 'cb', axis=0, tiled=True)  60.2 us
    all_gather x1, waiting for transfers between devices, shards(): lax.all_gather(input_weight, 'seq', axis=1, tiled=True)[0]  53.9 us
    all_gather x1, waiting for transfers between devices, shards(): value_piece = lax.all_gather(projected[2], 'seq', axis=1, tiled=True)  33.6 us
    all_gather x1, waiting for transfers between devices, shards(): key_piece = lax.all_gather(projected[1], 'seq', axis=1, tiled=True)  30.6 us
    unnamed x18, local copies, waits for them, and re-layouts  10.6 us
  transfers between devices with their start and end apart: 6, of which 6 were waited for; matrix products, arithmetic and copies ran while one was open for 9% of the time, Pallas kernels for 0%

commit v1 on v0

--- a/solution.py
+++ b/solution.py
@@ -73,7 +73,10 @@
     temporal = (hidden_f.reshape(row_count, width) + summed).astype(jnp.bfloat16)
     projected_in = jnp.dot(
         temporal,
-        lax.all_gather(input_weight, "seq", axis=1, tiled=True)[0],
+        jnp.concatenate(
+            jax.lax.all_to_all(jnp.stack([input_weight] * jax.lax.axis_size("seq")), "seq", 0, 0),
+            axis=1,
+        )[0],
         preferred_element_type=jnp.float32,
     )
     entry = jnp.take(embedding[0], codebook_ids.reshape(row_count), axis=0).astype(jnp.float32)

time: 420 us -> 439 us (1.045)
  waiting for transfers between devices: 327 us -> 335 us
  starting transfers between devices: 0.65 us -> 7.21 us
  local copies, waits for them, and re-layouts: 29.8 us -> 34.2 us
    all_gather x1 -> x0, waiting for transfers between devices: 53.9 us -> none  [shards(): lax.all_gather(input_weight, 'seq', axis=1, tiled=True)[0]]
    all_gather x1, waiting for transfers between devices: 33.6 us -> 67.7 us  [shards(): value_piece = lax.all_gather(projected[2], 'seq', axis=1, tiled=True)]
    all_gather x1, waiting for transfers between devices: 30.6 us -> 53.3 us  [shards(): key_piece = lax.all_gather(projected[1], 'seq', axis=1, tiled=True)]
    all_to_all x0 -> x1, starting transfers between devices: none -> 6.83 us  [shards(): jax.lax.all_to_all(jnp.stack([input_weight] * jax.lax.axis_size('seq')),...]
    unnamed x18 -> x20, local copies, waits for them, and re-layouts: 10.6 us -> 10.6 us
  transfers between devices with their start and end apart: 6 -> 6, of which waited for: 6 -> 5; matrix products, arithmetic and copies ran while one was open for 9% -> 11% of each run, Pallas kernels for 0% -> 0%
where the time goes in v1:
time: 439 us; the launch traced here: 438 us
  waiting for transfers between devices  335 us (76%)
  local copies, waits for them, and re-layouts  34.2 us (8%)
  matrix products  33.7 us (8%)
  between operations  14.1 us (3%)
  other arithmetic  13.8 us (3%)
  starting transfers between devices  7.21 us (2%)
    psum x1, waiting for transfers between devices, shards(): summed = lax.psum(term.astype(jnp.bfloat16), 'cb').astype(jnp.float32)  85.2 us
    all_gather x1, waiting for transfers between devices, shards(): key_piece = lax.all_gather(book_key[None], 'cb', axis=0, tiled=True)  68.8 us
    all_gather x1, waiting for transfers between devices, shards(): value_piece = lax.all_gather(projected[2], 'seq', axis=1, tiled=True)  67.7 us
    all_gather x1, waiting for transfers between devices, shards(): value_piece = lax.all_gather(book_value[None], 'cb', axis=0, tiled=True)  60.2 us
    all_gather x1, waiting for transfers between devices, shards(): key_piece = lax.all_gather(projected[1], 'seq', axis=1, tiled=True)  53.3 us
    unnamed x20, local copies, waits for them, and re-layouts  10.6 us
  transfers between devices with their start and end apart: 6, of which 5 were waited for; matrix products, arithmetic and copies ran while one was open for 11% of the time, Pallas kernels for 0%

profile of v1, /device:TPU:1, one launch (start us, length us, event | category | flops | bytes accessed | tf_op | source)
XLA Modules:
  0.0 438.3 jit_solution(11068968222931135475)
XLA Ops:
  7.2 0.0 all-gather.9.cloned.1.call-start
  7.2 2.2 multiply_reduce_fusion.2
  9.5 2.3 multiply_convert_fusion
  11.8 1.3 copy-done.5
  13.1 2.3 fusion.51
  15.5 0.7 copy.25
  16.2 0.0 all-gather.9.cloned.1.call-update
  16.2 0.0 all-gather.7.cloned.1.call-start
  16.3 2.9 fusion.45
  19.2 0.8 copy.24
  20.0 0.0 all-gather.7.cloned.1.call-update
  20.0 4.3 stack.2
  24.4 6.8 %all-to-all-start = ((bf16[16,1,256,1024]{3,2,1,0:T(8,128)(2,1)}), bf16[16,1,256,1024]{3,2,1,0:T(8,128)(2,1)}, u32[]{:S(2)}, u32[]{:S(2)}) async-start(bf16[16,1,256,1024]{3,2,1,0:T(8,128)(2,1)} %stack.2), calls=%async_computation | async-start | bytes 16777216 | tf_op jit(solution)/shard_map/all_to_all | solution.py:77
  31.2 0.0 all-reduce.2.cloned.1.call-start
  31.2 3.0 fusion.48
  34.3 0.2 iota_compare_fusion
  34.5 53.3 %all-gather.9.cloned.1.call-done = bf16[2,2048,2,128]{3,1,2,0:T(8,128)(2,1)} async-done(((bf16[2,128,2,128]{3,1,2,0:T(8,128)(2,1)}), bf16[2,2048,2,128]{3,1,2,0:T(8,128)(2,1)}) %all-gather.9.cloned.1.call-update) | async-done | bytes 2097168 | tf_op jit(solution)/shard_map/all_gather | solution.py:45
  87.8 2.6 fusion.1
  90.5 1.9 copy-done.3
  92.4 1.3 fusion.2
  93.6 67.7 %all-gather.7.cloned.1.call-done = bf16[2,2048,2,128]{1,3,2,0:T(8,128)(2,1)} async-done(((bf16[2,128,2,128]{1,3,2,0:T(8,128)(2,1)}), bf16[2,2048,2,128]{1,3,2,0:T(8,128)(2,1)}) %all-gather.7.cloned.1.call-update) | async-done | bytes 2097168 | tf_op jit(solution)/shard_map/all_gather | solution.py:46
  161.4 4.1 fusion.57
  165.5 0.1 copy.27
  165.7 2.0 convolution_convert_fusion
  167.7 0.0 all-reduce.2.cloned.1.call-update
  167.7 0.2 all-gather.11.cloned.1.call-start
  168.0 4.4 %gather_fusion = bf16[256,1024]{1,0:T(8,128)(2,1)S(1)} fusion(bf16[2048,1024]{1,0:T(8,128)(2,1)} %bitcast.96, s32[1024]{0:T(1024)S(1)} %pad_clamp_fusion), kind=kCustom, calls=%fused_computation | custom fusion | bytes 1049600 | tf_op jit(solution)/shard_map/jit(_take)/gather | solution.py:82
  172.4 85.2 %all-reduce.2.cloned.1.call-done = bf16[256,4096]{1,0:T(8,128)(2,1)} async-done(((bf16[256,4096]{1,0:T(8,128)(2,1)}), bf16[256,4096]{1,0:T(8,128)(2,1)}) %all-reduce.2.cloned.1.call-update) | async-done | bytes 2097168 | tf_op jit(solution)/shard_map/psum | solution.py:72
  257.6 3.7 fusion
  261.3 6.5 %fusion.60 = (f32[256]{0:T(256)S(1)}, bf16[256,1024]{1,0:T(8,128)(2,1)S(1)}) fusion(bf16[256,1024]{1,0:T(8,128)(2,1)S(1)} %gather_fusion, pred[256]{0:T(512)(128)(4,1)S(1)} %compare_and_fusion, bf16[256,4096]{1,0:T(8,128)(2,1)} %fusion, bf16[4096,1024]{1,0:T(8,128)(2,1)} %bitcast.11), kind=kOutput, calls=%fused_computation.50 | convolution fusion | flops 2149318400 | bytes 11535616 | tf_op jit(solution)/shard_map/dot_general | solution.py:74
  267.8 3.1 fusion.36
  270.9 0.0 all-gather.13.cloned.1.call-start
  271.0 3.2 fusion.39
  274.2 2.3 fusion.33
  276.6 0.2 copy.28
  276.8 0.1 bitcast_convert_fusion
  276.9 68.8 %all-gather.11.cloned.1.call-done = bf16[2048,1024]{1,0:T(8,128)(2,1)} async-done(((bf16[256,1024]{1,0:T(8,128)(2,1)}), bf16[2048,1024]{1,0:T(8,128)(2,1)}) %all-gather.11.cloned.1.call-update) | async-done | bytes 4194320 | tf_op jit(solution)/shard_map/all_gather | solution.py:98
  345.7 6.5 %copy.29 = bf16[2048,1024]{0,1:T(8,128)(2,1)} copy(bf16[2048,1024]{1,0:T(8,128)(2,1)} %all-gather.11.cloned.1.call-done) | data formatting | bytes 8388608 | tf_op jit(solution)/shard_map/all_gather | solution.py:98
  352.2 3.7 copy.47
  355.9 0.9 multiply_reduce_fusion.1
  356.8 0.1 fusion.67
  356.9 0.1 fusion.68
  357.1 60.2 %all-gather.13.cloned.1.call-done = bf16[2048,1024]{1,0:T(8,128)(2,1)} async-done(((bf16[256,1024]{1,0:T(8,128)(2,1)}), bf16[2048,1024]{1,0:T(8,128)(2,1)}) %all-gather.13.cloned.1.call-update) | async-done | bytes 4194320 | tf_op jit(solution)/shard_map/all_gather | solution.py:99
  417.3 6.5 %copy.30 = bf16[2048,1024]{0,1:T(8,128)(2,1)} copy(bf16[2048,1024]{1,0:T(8,128)(2,1)} %all-gather.13.cloned.1.call-done) | data formatting | bytes 8388608 | tf_op jit(solution)/shard_map/all_gather | solution.py:99
  423.8 3.7 copy.48
  427.5 2.6 multiply_reduce_fusion
  430.1 0.1 divide_convert_fusion
  430.2 1.5 fusion.30
  (31 shorter events, 0.2 us)
Async XLA Ops:
  7.2 158.5 %copy-start = (bf16[256,4096]{1,0:T(8,128)(2,1)S(1)}, bf16[256,4096]{1,0:T(8,128)(2,1)}, u32[]{:S(2)}) copy-start(bf16[256,4096]{1,0:T(8,128)(2,1)} %param.13) | copy-start | bytes 6291460
  7.2 80.6 %all-gather.9.cloned.1.call-start = ((), (), s32[]{:S(2)}) async-start(), calls=%async_computation.2 | async-start | bytes 2228224 | tf_op jit(solution)/shard_map/all_gather | solution.py:45
  11.8 1.3 copy-start.5
  15.5 4.6 %copy-start.6 = (bf16[1,256,1024]{2,1,0:T(8,128)(2,1)S(1)}, bf16[1,256,1024]{2,1,0:T(8,128)(2,1)}, u32[]{:S(2)}) copy-start(bf16[1,256,1024]{2,1,0:T(8,128)(2,1)} %param.16) | copy-start | bytes 1572868
  16.2 145.2 %all-gather.7.cloned.1.call-start = ((), (), s32[]{:S(2)}) async-start(), calls=%async_computation.1 | async-start | bytes 2228224 | tf_op jit(solution)/shard_map/all_gather | solution.py:46
  24.4 236.9 %all-to-all-start = ((bf16[16,1,256,1024]{3,2,1,0:T(8,128)(2,1)}), bf16[16,1,256,1024]{3,2,1,0:T(8,128)(2,1)}, u32[]{:S(2)}, u32[]{:S(2)}) async-start(bf16[16,1,256,1024]{3,2,1,0:T(8,128)(2,1)} %stack.2), calls=%async_computation | async-start | bytes 16777216 | tf_op jit(solution)/shard_map/all_to_all | solution.py:77
  31.2 226.4 %all-reduce.2.cloned.1.call-start = ((), (), s32[]{:S(2)}) async-start(), calls=%async_computation.3 | async-start | bytes 4194304 | tf_op jit(solution)/shard_map/psum | solution.py:72
  90.4 1.9 copy-start.3
  165.5 2.5 copy-start.7
  167.7 89.9 %copy-start.2 = (bf16[2,128,4096]{2,1,0:T(8,128)(2,1)S(1)}, bf16[2,128,4096]{2,1,0:T(8,128)(2,1)}, u32[]{:S(2)}) copy-start(bf16[2,128,4096]{2,1,0:T(8,128)(2,1)} %param.10) | copy-start | bytes 6291460
  167.7 178.0 %all-gather.11.cloned.1.call-start = ((), (), s32[]{:S(2)}) async-start(), calls=%async_computation.4 | async-start | bytes 4718592 | tf_op jit(solution)/shard_map/all_gather | solution.py:98
  261.3 6.5 %copy-start.8 = (f32[1,1024]{1,0:T(1,128)S(1)}, f32[1,1024]{1,0:T(1,128)}, u32[]{:S(2)}) copy-start(f32[1,1024]{1,0:T(1,128)} %param.17) | copy-start | bytes 12292
  270.9 146.3 %all-gather.13.cloned.1.call-start = ((), (), s32[]{:S(2)}) async-start(), calls=%async_computation.5 | async-start | bytes 4718592 | tf_op jit(solution)/shard_map/all_gather | solution.py:99
  427.4 2.8 copy-start.4
  427.5 4.3 copy-start.1
Sparse Core Ops, SparseCore 0:
  16.3 71.4 all-gather.8
  90.0 71.3 all-gather.6
  167.8 89.7 all-reduce.1
  271.1 74.6 all-gather.10
  347.9 69.2 all-gather.12
